TPU v7x, 512 devices: a whole 4x4x16 slice. The times are simulated.
512 devices in a mesh: tile: 32 (over z_lo, y, core), date: 16 (over z_hi, x).
Axes of the slice: x: 4, y: 4, z: 16 (z_hi: 4, z_lo: 4; z = z_hi * 4 + z_lo), core: 2. Of those that a mesh axis runs over, the one named last changes fastest.
Arguments:
- secondary: bfloat16 [16, 2, 3072, 1024], P('date', None, 'tile'), may hold values from -6 to 6
- primary: bfloat16 [2, 3072, 1024], P(None, 'tile', 'date'), may hold values from -6 to 6
- margin_mask: int32 [3072], P('tile'), may hold values from 0 to 1, as said below
- az_off: int32 [16, 32], P('date', 'tile'), may hold values from -16 to 16
- rg_off: int32 [16, 32], P('date', 'tile'), may hold values from -16 to 16
- az_frac: float32 [16, 32], P('date', 'tile'), may hold values from 0 to 1
- rg_frac: float32 [16, 32], P('date', 'tile'), may hold values from 0 to 1
Outputs:
- looks: float32 [16, 2, 1536, 128], P('date', None, 'tile')
Inputs may be any that keep to these rules, and one draw needn't show every extreme that they name: `margin_mask`: ones lie only in the last 64 rows of each tile of 96 rows, and the last row of every tile is 1.
All inputs are finite; a program needn't handle non-finite values.
Results may differ from a plain program's by a relative error of at most 0.017.
Values may be sent and summed in bfloat16 or wider, within the bound.
A program may use at most 64 MiB of HBM per device.

v0:
```python
import jax
import jax.numpy as jnp
from jax import lax
from jax.sharding import PartitionSpec as P

KA = 16
LAG = 64
LA = 2
LR = 8


def padded(block, sides, width):
    for axis, dim in sides:
        count = lax.axis_size(axis)
        forward = [(i, i + 1) for i in range(count - 1)]
        backward = [(target, source) for source, target in forward]
        low = lax.ppermute(
            lax.slice_in_dim(block, block.shape[dim] - width, None, axis=dim), axis, forward
        )
        high = lax.ppermute(lax.slice_in_dim(block, 0, width, axis=dim), axis, backward)
        block = jnp.concatenate([low, block, high], axis=dim)
    return block


def passed_along(value, axis, steps):
    count = lax.axis_size(axis)
    initial, last = (max(0, -steps), min(count, count - steps))
    return lax.ppermute(value, axis, [(source, source + steps) for source in range(initial, last)])


def window(dist):
    return jnp.sinc(dist) * (0.5 + 0.5 * jnp.cos(jnp.pi * dist / 4.0))


def band_taps(offset, frac):
    inside = (offset >= -3) & (offset <= 4)
    return jnp.where(inside, window(offset.astype(jnp.float32) - frac), 0.0).astype(jnp.bfloat16)


def multilook(values):
    depth, rows_n, cols_n = values.shape
    return values.reshape(depth, rows_n // LA, LA, cols_n // LR, LR).mean(axis=(2, 4))


def shards(secondary, primary, margin_mask, az_off, rg_off, az_frac, rg_frac):
    rim_rows = KA + 4
    block_cols = 256
    image = secondary[0]
    rows_n = image.shape[1]
    cols_n = image.shape[2]
    extended = padded(image, (("tile", 1),), rim_rows)
    row_out = lax.broadcasted_iota(jnp.int32, (rows_n, rows_n + 2 * rim_rows), 0)
    row_in = lax.broadcasted_iota(jnp.int32, (rows_n, rows_n + 2 * rim_rows), 1)
    azim_taps = band_taps(row_in - row_out - az_off[0, 0] - rim_rows, az_frac[0, 0])
    azim = jnp.einsum(
        "im,kmc->kic", azim_taps, extended, preferred_element_type=jnp.float32
    ).astype(jnp.bfloat16)
    blocks_n = cols_n // block_cols
    col_pad = jnp.pad(azim, ((0, 0), (0, 0), (block_cols // 2, block_cols // 2)))
    pieces = col_pad.reshape(2, rows_n, blocks_n + 1, block_cols)
    inputs = jnp.concatenate([pieces[:, :, :-1], pieces[:, :, 1:]], axis=3)
    col_in = lax.broadcasted_iota(jnp.int32, (2 * block_cols, block_cols), 0)
    col_out = lax.broadcasted_iota(jnp.int32, (2 * block_cols, block_cols), 1)
    range_taps = band_taps(col_in - block_cols // 2 - col_out - rg_off[0, 0], rg_frac[0, 0])
    resampled = jnp.einsum("kibm,mn->kibn", inputs, range_taps, preferred_element_type=jnp.float32)
    resampled = resampled.reshape(2, rows_n, cols_n).astype(jnp.bfloat16)
    prim = lax.all_gather(primary, "date", axis=2, tiled=True)[None]
    moved = resampled[None]
    sec_f = moved.astype(jnp.float32)
    prim_f = prim.astype(jnp.float32)
    ifg_re = prim_f[:, 0] * sec_f[:, 0] + prim_f[:, 1] * sec_f[:, 1]
    ifg_im = prim_f[:, 1] * sec_f[:, 0] - prim_f[:, 0] * sec_f[:, 1]
    interf = jnp.stack((ifg_re, ifg_im), axis=1)
    upcoming = passed_along(interf[:, :, :LAG, :], "tile", -1)
    later = jnp.concatenate([interf[:, :, LAG:, :], upcoming], axis=2)
    l_re = later[:, 0]
    l_im = later[:, 1]
    weight = margin_mask.astype(jnp.float32)[None, :, None]
    e_re = jnp.sum(weight * (ifg_re * l_re + ifg_im * l_im), axis=(1, 2))
    e_im = jnp.sum(weight * (ifg_im * l_re - ifg_re * l_im), axis=(1, 2))
    power = jnp.sum(
        weight * 0.5 * (ifg_re * ifg_re + ifg_im * ifg_im + l_re * l_re + l_im * l_im), axis=(1, 2)
    )
    count = jnp.zeros_like(e_re) + jnp.sum(margin_mask.astype(jnp.float32)) * interf.shape[3]
    stats = jnp.stack((e_re, e_im, power, count), axis=1)
    totals = lax.psum(stats, "tile")
    magnitude = jnp.sqrt(totals[:, 0] * totals[:, 0] + totals[:, 1] * totals[:, 1])
    floor_val = (totals[:, 2] + 1e-06) / jnp.sqrt(jnp.maximum(totals[:, 3], 1.0))
    denom = jnp.maximum(magnitude, floor_val)
    u_re = (totals[:, 0] / denom)[:, None, None]
    u_im = (totals[:, 1] / denom)[:, None, None]
    c_re = multilook(ifg_re * u_re + ifg_im * u_im)
    c_im = multilook(ifg_im * u_re - ifg_re * u_im)
    result = jnp.stack((c_re, c_im), axis=1)
    return result


def solution(mesh):
    return jax.shard_map(
        shards,
        mesh=mesh,
        in_specs=(
            P("date", None, "tile", None),
            P(None, "tile", "date"),
            P("tile"),
            P("date", "tile"),
            P("date", "tile"),
            P("date", "tile"),
            P("date", "tile"),
        ),
        out_specs=P("date", None, "tile", None),
        check_vma=False,
    )
```

profile of v0, /device:TPU:1, one launch (start us, length us, event | category | flops | bytes accessed | tf_op | source)
XLA Modules:
  0.0 181.6 jit_solution(2312911935924852726)
XLA Ops:
  0.0 1.0 fusion.116
  1.0 4.6 %collective-permute-start = (bf16[2,20,1024]{2,1,0:T(8,128)(2,1)S(1)}, bf16[2,20,1024]{2,1,0:T(8,128)(2,1)S(1)}, u32[]{:S(2)}, u32[]{:S(2)}) collective-permute-start(bf16[2,20,1024]{2,1,0:T(8,128)(2,1)S(1)} %get-tuple-element.14), channel_id=1, source_target_pairs={{0,16},{16,32},{32,48},{48,64},{64,80},{80,96},{96,112},{112,128},... | collective-permute-start | bytes 245768 | tf_op jit(solution)/shard_map/ppermute | solution.py:17
  5.6 5.5 %collective-permute-start.1 = (bf16[2,20,1024]{2,1,0:T(8,128)(2,1)S(1)}, bf16[2,20,1024]{2,1,0:T(8,128)(2,1)S(1)}, u32[]{:S(2)}, u32[]{:S(2)}) collective-permute-start(bf16[2,20,1024]{2,1,0:T(8,128)(2,1)S(1)} %get-tuple-element.15), channel_id=1, source_target_pairs={{16,0},{32,16},{48,32},{64,48},{80,64},{96,80},{112,96},{128,112},... | collective-permute-start | bytes 245768 | tf_op jit(solution)/shard_map/ppermute | solution.py:20
  13.7 0.8 copy.15
  14.5 55.4 %all_gather.3 = bf16[2,96,1024]{1,0,2:T(2,128)(2,1)S(1)} all-gather(bf16[2,96,64]{1,0,2:T(2,128)(2,1)S(1)} %copy.15), channel_id=1, replica_groups=mesh['tile'=32,'date'=16] {'date'}, dimensions={2}, use_global_device_ids=true | all-gather | bytes 417792 | tf_op jit(solution)/shard_map/all_gather | solution.py:67
  69.9 0.4 copy.16
  70.3 0.1 bitcast_convert_fusion
  70.4 0.6 fusion.1
  71.1 0.3 copy.24
  71.3 0.1 pad.4.clone
  71.5 0.2 fusion.115
  71.7 0.2 copy.22
  71.9 0.2 copy.23
  72.1 2.9 %fusion = f32[2,96,4,256]{3,1,2,0:T(8,128)S(1)} fusion(bf16[2,96,4,256]{3,1,2,0:T(8,128)(2,1)S(1)} %copy.23, bf16[2,96,4,256]{3,1,2,0:T(8,128)(2,1)S(1)} %copy.22, f32[]{:T(128)} %bitcast.51, s32[]{:T(128)} %bitcast.49, s32[512]{0:T(512)S(1)} %iota_add_fusion), kind=kOutput, calls=%fused_computation.2 | convolution fusion | flops 209321984 | bytes 1574920 | tf_op jit(solution)/shard_map/kibm,mn->kibn/dot_general | solution.py:65
  75.0 0.5 copy.20
  75.5 0.4 reshape.581
  75.9 0.0 copy-start.1
  75.9 0.2 multiply_subtract_fusion.1
  76.1 3.9 %collective-permute-start.2 = (f32[1,2,64,1024]{3,2,1,0:T(8,128)S(1)}, f32[1,2,64,1024]{3,2,1,0:T(8,128)S(1)}, u32[]{:S(2)}, u32[]{:S(2)}) collective-permute-start(f32[1,2,64,1024]{3,2,1,0:T(8,128)S(1)} %pad_maximum_fusion.1), channel_id=1, source_target_pairs={{16,0},{32,16},{48,32},{64,48},{80,64},{96,80},{112,96},{128,112},... | collective-permute-start | bytes 1572872 | tf_op jit(solution)/shard_map/ppermute | solution.py:28
  80.0 0.6 broadcast_multiply_fusion
  81.3 12.3 %collective-permute-done.2 = f32[1,2,64,1024]{3,2,1,0:T(8,128)S(1)} collective-permute-done((f32[1,2,64,1024]{3,2,1,0:T(8,128)S(1)}, f32[1,2,64,1024]{3,2,1,0:T(8,128)S(1)}, u32[]{:S(2)}, u32[]{:S(2)}) %collective-permute-start.2) | collective-permute-done | bytes 524320 | tf_op jit(solution)/shard_map/ppermute | solution.py:28
  93.6 0.1 fusion.2
  93.7 1.0 fusion.29
  94.7 2.0 %pad_maximum_fusion.3 = f32[1,4]{1,0:T(1,128)S(1)} fusion(f32[1,1]{1,0:T(1,128)} %bitcast.18, f32[1,1]{1,0:T(1,128)} %bitcast.17, f32[1,1]{1,0:T(1,128)} %bitcast.15, f32[1,1]{1,0:T(1,128)} %bitcast.13), kind=kLoop, calls=%fused_computation.124 | loop fusion | flops 12 | bytes 32 | tf_op jit(solution)/shard_map/stack | solution.py:85
  96.6 61.0 %psum.7 = f32[1,4]{1,0:T(1,128)S(1)} all-reduce(f32[1,4]{1,0:T(1,128)S(1)} %pad_maximum_fusion.3), channel_id=1, replica_groups=mesh['tile'=32,'date'=16] {'tile'}, use_global_device_ids=true, to_apply=%region_4.5 | all-reduce | flops 4 | bytes 32 | tf_op jit(solution)/shard_map/psum | solution.py:86
  157.7 0.6 fusion.117
  163.6 0.1 multiply_add_fusion.1
  163.7 5.0 %add.275 = f32[48,2,128,8]{3,2,1,0:T(8,128)} reshape(f32[1,1,96,1024]{3,2,1,0:T(8,128)S(1)} %get-tuple-element.10) | data formatting | bytes 786432 | tf_op jit(solution)/shard_map/add | solution.py:92
  168.6 5.0 %sub.152 = f32[48,2,128,8]{3,2,1,0:T(8,128)} reshape(f32[1,1,96,1024]{3,2,1,0:T(8,128)S(1)} %get-tuple-element.11) | data formatting | bytes 786432 | tf_op jit(solution)/shard_map/sub | solution.py:93
  173.6 3.7 %reduce_sum.58 = f32[48,128]{1,0:T(8,128)S(1)} reduce(f32[48,2,128,8]{3,2,1,0:T(8,128)} %add.275, f32[]{:T(128)} %constant.55.clone.1), dimensions={1,3}, to_apply=%region_5.6 | reduce | flops 92160 | bytes 417796 | tf_op jit(solution)/shard_map/reduce_sum | solution.py:42
  177.3 3.7 %reduce_sum.59 = f32[48,128]{1,0:T(8,128)S(1)} reduce(f32[48,2,128,8]{3,2,1,0:T(8,128)} %sub.152, f32[]{:T(128)} %constant.55.clone.1), dimensions={1,3}, to_apply=%region_6.7 | reduce | flops 92160 | bytes 417796 | tf_op jit(solution)/shard_map/reduce_sum | solution.py:42
  181.0 0.6 pad_maximum_fusion.2
  (9 shorter events, 0.1 us)
Async XLA Ops:
  0.0 70.4 %copy-start = (bf16[1,2,96,1024]{3,2,1,0:T(8,128)(2,1)S(1)}, bf16[1,2,96,1024]{3,2,1,0:T(8,128)(2,1)}, u32[]{:S(2)}) copy-start(bf16[1,2,96,1024]{3,2,1,0:T(8,128)(2,1)} %param.7) | copy-start | bytes 1179652
  1.0 69.4 %collective-permute-start = (bf16[2,20,1024]{2,1,0:T(8,128)(2,1)S(1)}, bf16[2,20,1024]{2,1,0:T(8,128)(2,1)S(1)}, u32[]{:S(2)}, u32[]{:S(2)}) collective-permute-start(bf16[2,20,1024]{2,1,0:T(8,128)(2,1)S(1)} %get-tuple-element.14), channel_id=1, source_target_pairs={{0,16},{16,32},{32,48},{48,64},{64,80},{80,96},{96,112},{112,128},... | collective-permute-start | bytes 245768 | tf_op jit(solution)/shard_map/ppermute | solution.py:17
  5.6 64.8 %collective-permute-start.1 = (bf16[2,20,1024]{2,1,0:T(8,128)(2,1)S(1)}, bf16[2,20,1024]{2,1,0:T(8,128)(2,1)S(1)}, u32[]{:S(2)}, u32[]{:S(2)}) collective-permute-start(bf16[2,20,1024]{2,1,0:T(8,128)(2,1)S(1)} %get-tuple-element.15), channel_id=1, source_target_pairs={{16,0},{32,16},{48,32},{64,48},{80,64},{96,80},{112,96},{128,112},... | collective-permute-start | bytes 245768 | tf_op jit(solution)/shard_map/ppermute | solution.py:20
  75.9 4.1 %copy-start.1 = (s32[96]{0:T(128)S(1)}, s32[96]{0:T(128)}, u32[]{:S(2)}) copy-start(s32[96]{0:T(128)} %param.9) | copy-start | bytes 1156
  76.1 17.5 %collective-permute-start.2 = (f32[1,2,64,1024]{3,2,1,0:T(8,128)S(1)}, f32[1,2,64,1024]{3,2,1,0:T(8,128)S(1)}, u32[]{:S(2)}, u32[]{:S(2)}) collective-permute-start(f32[1,2,64,1024]{3,2,1,0:T(8,128)S(1)} %pad_maximum_fusion.1), channel_id=1, source_target_pairs={{16,0},{32,16},{48,32},{64,48},{80,64},{96,80},{112,96},{128,112},... | collective-permute-start | bytes 1572872 | tf_op jit(solution)/shard_map/ppermute | solution.py:28
where the time goes:
time: 182 us
  blocking collectives  116 us (64%)
  local copies, waits for them, and re-layouts  14.7 us (8%)
  starting transfers between devices  13.9 us (8%)
  waiting for transfers between devices  12.3 us (7%)
  other arithmetic  12 us (7%)
  between operations  8.73 us (5%)
  matrix products  3.52 us (2%)
    psum x1, blocking collectives, shards(): totals = lax.psum(stats, 'tile')  61 us
    all_gather x1, blocking collectives, shards(): prim = lax.all_gather(primary, 'date', axis=2, tiled=True)[None]  55.4 us
    ppermute x1, waiting for transfers between devices, passed_along(): lax.ppermute(value, axis, [(source, source + steps) for source in range(i...  12.3 us
    reduce_sum x2, other arithmetic, multilook(): values.reshape(depth, rows_n // LA, LA, cols_n // LR, LR).mean(axis=(2, 4))  7.34 us
    ppermute x1, starting transfers between devices, padded(): lax.ppermute(lax.slice_in_dim(block, 0, width, axis=dim), axis, backward)  5.46 us
    sub x1, local copies, waits for them, and re-layouts, shards(): c_im = multilook(ifg_im * u_re - ifg_re * u_im)  4.97 us
    add x1, local copies, waits for them, and re-layouts, shards(): c_re = multilook(ifg_re * u_re + ifg_im * u_im)  4.95 us
    ppermute x1, starting transfers between devices, padded(): lax.ppermute(lax.slice_in_dim(block, block.shape[dim] - width, None, axis...  4.58 us
  transfers between devices with their start and end apart: 3, of which 1 were waited for; matrix products, arithmetic and copies ran while one was open for 1% of the time, Pallas kernels for 0%

commit v1 on v0

--- a/solution.py
+++ b/solution.py
@@ -83,7 +83,8 @@
     )
     count = jnp.zeros_like(e_re) + jnp.sum(margin_mask.astype(jnp.float32)) * interf.shape[3]
     stats = jnp.stack((e_re, e_im, power, count), axis=1)
-    totals = lax.psum(stats, "tile")
+    parts = lax.all_gather(stats, "tile")
+    totals = jnp.sum(parts, axis=0)
     magnitude = jnp.sqrt(totals[:, 0] * totals[:, 0] + totals[:, 1] * totals[:, 1])
     floor_val = (totals[:, 2] + 1e-06) / jnp.sqrt(jnp.maximum(totals[:, 3], 1.0))
     denom = jnp.maximum(magnitude, floor_val)

time: 182 us -> 159 us (0.87)
  blocking collectives: 116 us -> 93.3 us
    psum x1 -> x0, blocking collectives: 61 us -> none  [shards(): totals = lax.psum(stats, 'tile')]
    all_gather x0 -> x1, blocking collectives: none -> 37.9 us  [shards(): parts = lax.all_gather(stats, 'tile')]
    another operation x1 -> x0, other arithmetic: 1.95 us -> none  [shards(): stats = jnp.stack((e_re, e_im, power, count), axis=1)]
    unnamed x0 -> x1, other arithmetic: none -> 1.95 us
where the time goes in v1:
time: 159 us
  blocking collectives  93.3 us (59%)
  local copies, waits for them, and re-layouts  14.7 us (9%)
  starting transfers between devices  13.9 us (9%)
  waiting for transfers between devices  12.3 us (8%)
  other arithmetic  12 us (8%)
  between operations  8.73 us (5%)
  matrix products  3.52 us (2%)
    all_gather x1, blocking collectives, shards(): prim = lax.all_gather(primary, 'date', axis=2, tiled=True)[None]  55.4 us
    all_gather x1, blocking collectives, shards(): parts = lax.all_gather(stats, 'tile')  37.9 us
    ppermute x1, waiting for transfers between devices, passed_along(): lax.ppermute(value, axis, [(source, source + steps) for source in range(i...  12.3 us
    reduce_sum x2, other arithmetic, multilook(): values.reshape(depth, rows_n // LA, LA, cols_n // LR, LR).mean(axis=(2, 4))  7.33 us
    ppermute x1, starting transfers between devices, padded(): lax.ppermute(lax.slice_in_dim(block, 0, width, axis=dim), axis, backward)  5.46 us
    add x1, local copies, waits for them, and re-layouts, shards(): c_re = multilook(ifg_re * u_re + ifg_im * u_im)  5 us
    sub x1, local copies, waits for them, and re-layouts, shards(): c_im = multilook(ifg_im * u_re - ifg_re * u_im)  5 us
    ppermute x1, starting transfers between devices, padded(): lax.ppermute(lax.slice_in_dim(block, block.shape[dim] - width, None, axis...  4.58 us
  transfers between devices with their start and end apart: 3, of which 1 were waited for; matrix products, arithmetic and copies ran while one was open for 1% of the time, Pallas kernels for 0%

profile of v1, /device:TPU:1, one launch (start us, length us, event | category | flops | bytes accessed | tf_op | source)
XLA Modules:
  0.0 158.6 jit_solution(8683836538032469670)
XLA Ops:
  0.0 1.0 fusion.116
  1.0 4.6 %collective-permute-start = (bf16[2,20,1024]{2,1,0:T(8,128)(2,1)S(1)}, bf16[2,20,1024]{2,1,0:T(8,128)(2,1)S(1)}, u32[]{:S(2)}, u32[]{:S(2)}) collective-permute-start(bf16[2,20,1024]{2,1,0:T(8,128)(2,1)S(1)} %get-tuple-element.14), channel_id=1, source_target_pairs={{0,16},{16,32},{32,48},{48,64},{64,80},{80,96},{96,112},{112,128},... | collective-permute-start | bytes 245768 | tf_op jit(solution)/shard_map/ppermute | solution.py:17
  5.6 5.5 %collective-permute-start.1 = (bf16[2,20,1024]{2,1,0:T(8,128)(2,1)S(1)}, bf16[2,20,1024]{2,1,0:T(8,128)(2,1)S(1)}, u32[]{:S(2)}, u32[]{:S(2)}) collective-permute-start(bf16[2,20,1024]{2,1,0:T(8,128)(2,1)S(1)} %get-tuple-element.15), channel_id=1, source_target_pairs={{16,0},{32,16},{48,32},{64,48},{80,64},{96,80},{112,96},{128,112},... | collective-permute-start | bytes 245768 | tf_op jit(solution)/shard_map/ppermute | solution.py:20
  13.7 0.8 copy.15
  14.5 55.4 %all_gather.9 = bf16[2,96,1024]{1,0,2:T(2,128)(2,1)S(1)} all-gather(bf16[2,96,64]{1,0,2:T(2,128)(2,1)S(1)} %copy.15), channel_id=1, replica_groups=mesh['tile'=32,'date'=16] {'date'}, dimensions={2}, use_global_device_ids=true | all-gather | bytes 417792 | tf_op jit(solution)/shard_map/all_gather | solution.py:67
  69.9 0.4 copy.16
  70.3 0.1 bitcast_convert_fusion
  70.4 0.6 fusion.1
  71.1 0.3 copy.24
  71.3 0.1 pad.4.clone
  71.5 0.2 fusion.115
  71.7 0.2 copy.22
  71.9 0.2 copy.23
  72.1 2.9 %fusion = f32[2,96,4,256]{3,1,2,0:T(8,128)S(1)} fusion(bf16[2,96,4,256]{3,1,2,0:T(8,128)(2,1)S(1)} %copy.23, bf16[2,96,4,256]{3,1,2,0:T(8,128)(2,1)S(1)} %copy.22, f32[]{:T(128)} %bitcast.54, s32[]{:T(128)} %bitcast.52, s32[512]{0:T(512)S(1)} %iota_add_fusion), kind=kOutput, calls=%fused_computation.2 | convolution fusion | flops 209321984 | bytes 1574920 | tf_op jit(solution)/shard_map/kibm,mn->kibn/dot_general | solution.py:65
  75.0 0.5 copy.20
  75.5 0.4 reshape.582
  75.9 0.2 multiply_subtract_fusion.1
  76.1 3.9 %collective-permute-start.2 = (f32[1,2,64,1024]{3,2,1,0:T(8,128)S(1)}, f32[1,2,64,1024]{3,2,1,0:T(8,128)S(1)}, u32[]{:S(2)}, u32[]{:S(2)}) collective-permute-start(f32[1,2,64,1024]{3,2,1,0:T(8,128)S(1)} %pad_maximum_fusion.1), channel_id=1, source_target_pairs={{16,0},{32,16},{48,32},{64,48},{80,64},{96,80},{112,96},{128,112},... | collective-permute-start | bytes 1572872 | tf_op jit(solution)/shard_map/ppermute | solution.py:28
  80.0 0.6 broadcast_multiply_fusion
  81.3 12.3 %collective-permute-done.2 = f32[1,2,64,1024]{3,2,1,0:T(8,128)S(1)} collective-permute-done((f32[1,2,64,1024]{3,2,1,0:T(8,128)S(1)}, f32[1,2,64,1024]{3,2,1,0:T(8,128)S(1)}, u32[]{:S(2)}, u32[]{:S(2)}) %collective-permute-start.2) | collective-permute-done | bytes 524320 | tf_op jit(solution)/shard_map/ppermute | solution.py:28
  93.6 0.1 fusion.2
  93.7 1.0 fusion.29
  94.7 2.0 %maximum_bitcast_fusion = f32[1,1,4]{2,1,0:T(1,128)S(1)} fusion(f32[1,1]{1,0:T(1,128)} %bitcast.18, f32[1,1]{1,0:T(1,128)} %bitcast.17, f32[1,1]{1,0:T(1,128)} %bitcast.15, f32[1,1]{1,0:T(1,128)} %bitcast.13), kind=kLoop, calls=%fused_computation.124 | loop fusion | flops 12 | bytes 32
  96.6 37.9 %all-gather.1 = f32[32,1,4]{2,1,0:T(1,128)S(1)} all-gather(f32[1,1,4]{2,1,0:T(1,128)S(1)} %maximum_bitcast_fusion), channel_id=2, replica_groups=mesh['tile'=32,'date'=16] {'tile'}, dimensions={0}, use_global_device_ids=true | all-gather | bytes 528 | tf_op jit(solution)/shard_map/all_gather | solution.py:86
  134.5 0.1 reduce.8
  134.6 0.6 fusion.117
  140.5 0.1 multiply_add_fusion.1
  140.6 5.0 %add.273 = f32[48,2,128,8]{3,2,1,0:T(8,128)} reshape(f32[1,1,96,1024]{3,2,1,0:T(8,128)S(1)} %get-tuple-element.10) | data formatting | bytes 786432 | tf_op jit(solution)/shard_map/add | solution.py:93
  145.6 3.7 %reduce_sum.71 = f32[48,128]{1,0:T(8,128)S(1)} reduce(f32[48,2,128,8]{3,2,1,0:T(8,128)} %add.273, f32[]{:T(128)} %constant.55.clone.1), dimensions={1,3}, to_apply=%region_5.6 | reduce | flops 92160 | bytes 417796 | tf_op jit(solution)/shard_map/reduce_sum | solution.py:42
  149.3 5.0 %sub.152 = f32[48,2,128,8]{3,2,1,0:T(8,128)} reshape(f32[1,1,96,1024]{3,2,1,0:T(8,128)S(1)} %get-tuple-element.11) | data formatting | bytes 786432 | tf_op jit(solution)/shard_map/sub | solution.py:94
  154.3 3.7 %reduce_sum.72 = f32[48,128]{1,0:T(8,128)S(1)} reduce(f32[48,2,128,8]{3,2,1,0:T(8,128)} %sub.152, f32[]{:T(128)} %constant.55.clone.1), dimensions={1,3}, to_apply=%region_6.7 | reduce | flops 92160 | bytes 417796 | tf_op jit(solution)/shard_map/reduce_sum | solution.py:42
  157.9 0.6 pad_maximum_fusion.2
  (10 shorter events, 0.1 us)
Async XLA Ops:
  0.0 70.4 %copy-start = (bf16[1,2,96,1024]{3,2,1,0:T(8,128)(2,1)S(1)}, bf16[1,2,96,1024]{3,2,1,0:T(8,128)(2,1)}, u32[]{:S(2)}) copy-start(bf16[1,2,96,1024]{3,2,1,0:T(8,128)(2,1)} %param.7) | copy-start | bytes 1179652
  1.0 69.4 %collective-permute-start = (bf16[2,20,1024]{2,1,0:T(8,128)(2,1)S(1)}, bf16[2,20,1024]{2,1,0:T(8,128)(2,1)S(1)}, u32[]{:S(2)}, u32[]{:S(2)}) collective-permute-start(bf16[2,20,1024]{2,1,0:T(8,128)(2,1)S(1)} %get-tuple-element.14), channel_id=1, source_target_pairs={{0,16},{16,32},{32,48},{48,64},{64,80},{80,96},{96,112},{112,128},... | collective-permute-start | bytes 245768 | tf_op jit(solution)/shard_map/ppermute | solution.py:17
  5.6 64.8 %collective-permute-start.1 = (bf16[2,20,1024]{2,1,0:T(8,128)(2,1)S(1)}, bf16[2,20,1024]{2,1,0:T(8,128)(2,1)S(1)}, u32[]{:S(2)}, u32[]{:S(2)}) collective-permute-start(bf16[2,20,1024]{2,1,0:T(8,128)(2,1)S(1)} %get-tuple-element.15), channel_id=1, source_target_pairs={{16,0},{32,16},{48,32},{64,48},{80,64},{96,80},{112,96},{128,112},... | collective-permute-start | bytes 245768 | tf_op jit(solution)/shard_map/ppermute | solution.py:20
  75.9 4.1 %copy-start.1 = (s32[96]{0:T(128)S(1)}, s32[96]{0:T(128)}, u32[]{:S(2)}) copy-start(s32[96]{0:T(128)} %param.9) | copy-start | bytes 1156
  76.1 17.5 %collective-permute-start.2 = (f32[1,2,64,1024]{3,2,1,0:T(8,128)S(1)}, f32[1,2,64,1024]{3,2,1,0:T(8,128)S(1)}, u32[]{:S(2)}, u32[]{:S(2)}) collective-permute-start(f32[1,2,64,1024]{3,2,1,0:T(8,128)S(1)} %pad_maximum_fusion.1), channel_id=1, source_target_pairs={{16,0},{32,16},{48,32},{64,48},{80,64},{96,80},{112,96},{128,112},... | collective-permute-start | bytes 1572872 | tf_op jit(solution)/shard_map/ppermute | solution.py:28
